TPU v7x, 32 devices: a whole 2x2x4 slice. The times are simulated.
32 devices in a mesh: mem: 8 (over y, x, core), band: 4 (over z).
Axes of the slice: x: 2, y: 2, z: 4, core: 2. Of those that a mesh axis runs over, the one named last changes fastest.
Arguments:
- ensemble: bfloat16 [256, 3, 240, 160], P('mem', None, 'band'), may hold values from -8 to 8, as said below
- layer_depth: float32 [240, 160], P('band'), may hold values from 0.5 to 2
- observed_cell: int32 [8, 8, 512], P('mem', 'band'), may hold values from 0 to 1799
- observed_value: float32 [8, 8, 512], P('mem', 'band'), may hold values from -6 to 6
- error_variance: float32 [8, 8, 512], P('mem', 'band'), may hold values from 4 to 64
- observed_count: int32 [8, 8], P('mem', 'band'), may hold values from 256 to 512, as said below
Outputs:
- analysis: bfloat16 [256, 3, 240, 160], P('mem', None, 'band')
Inputs may be any that keep to these rules, and one draw needn't show every extreme that they name: `ensemble`: the forecast members scatter around a common state. `observed_count`: some tile holds 512 observations; the slots from the count on are unused.
All inputs are finite; a program needn't handle non-finite values.
Results may differ from a plain program's by a relative error of at most 0.0051.
The roundings to bfloat16 on the way count: a program that leaves them out, or rounds other values in their place, can miss the bound.
Values may be sent and summed in bfloat16 or wider, within the bound.
No kernel may reach another device: no remote copies, remote signals or barrier semaphores. Data moves between devices by JAX's collectives and lax.ppermute only.
A program may use at most 128 MiB of HBM per device.

v0:
```python
import math
import jax
import jax.numpy as jnp
from jax import lax
from jax.sharding import PartitionSpec as P

SWEEPS = 5
half_step = 0.1
coriolis_scale = 0.3
neighbour_weight = 0.75


def padded_2(cells, sides, width):
    for axis, dim in sides:
        count = lax.axis_size(axis)
        head = lax.slice_in_dim(cells, 0, width, axis=dim)
        tail = lax.slice_in_dim(cells, cells.shape[dim] - width, cells.shape[dim], axis=dim)
        cells = jnp.concatenate(
            [
                lax.ppermute(tail, axis, [(i, (i + 1) % count) for i in range(count)]),
                cells,
                lax.ppermute(head, axis, [((i + 1) % count, i) for i in range(count)]),
            ],
            axis=dim,
        )
    return cells


def north_south(source):
    widths = [(0, 0)] * (source.ndim - 1) + [(1, 1)]
    padded = jnp.pad(source, widths)
    return padded[..., 2:] - padded[..., :-2]


def coriolis(latitudes):
    position = jnp.arange(latitudes, dtype=jnp.float32)
    return coriolis_scale * jnp.sin(math.pi * ((position + 0.5) / latitudes - 0.5))


def newton_schulz(starting):
    identity = jnp.eye(starting.shape[-1], dtype=starting.dtype)
    root_part = starting
    inverse_root = jnp.broadcast_to(identity, starting.shape)
    for sweep_index in range(SWEEPS):
        product = jnp.einsum(
            "tij,tjk->tik", inverse_root, root_part, precision=lax.Precision.HIGHEST
        )
        middle = 1.5 * identity - 0.5 * product
        root_part = jnp.einsum("tij,tjk->tik", root_part, middle, precision=lax.Precision.HIGHEST)
        inverse_root = jnp.einsum(
            "tij,tjk->tik", middle, inverse_root, precision=lax.Precision.HIGHEST
        )
    return inverse_root


def on_device(ensemble, layer_depth, observed_cell, observed_value, error_variance, observed_count):
    block_members = ensemble.shape[0]
    columns = ensemble.shape[2]
    latitudes = ensemble.shape[3]
    strips = lax.axis_size("mem")
    members = block_members * strips
    strip_rows = latitudes // strips
    tile_count = observed_cell.shape[1]
    tile_columns = columns // tile_count
    slot_count = observed_cell.shape[2]
    tile_cells = 3 * tile_columns * strip_rows
    height = ensemble[:, 0].astype(jnp.float32)
    eastward = ensemble[:, 1].astype(jnp.float32)
    northward = ensemble[:, 2].astype(jnp.float32)
    turning = coriolis(latitudes)
    flux_east = (layer_depth * eastward).astype(jnp.bfloat16)
    flux_north = (layer_depth * northward).astype(jnp.bfloat16)
    east_margin = padded_2(flux_east, (("band", 1),), 1)
    east_west = east_margin[:, 2:].astype(jnp.float32) - east_margin[:, :-2].astype(jnp.float32)
    north_local = lax.optimization_barrier(flux_north).astype(jnp.float32)
    raised = height - half_step * (east_west + north_south(north_local))
    surface_elevation_cast = raised.astype(jnp.bfloat16)
    height_margin = padded_2(surface_elevation_cast, (("band", 1),), 1)
    margin_wide = height_margin.astype(jnp.float32)
    height_inner = margin_wide[:, 1:-1]
    revised_zonal_velocity = (
        eastward + turning * northward - half_step * (margin_wide[:, 2:] - margin_wide[:, :-2])
    )
    revised_meridional_velocity = (
        northward - turning * eastward - half_step * north_south(height_inner)
    )
    advance_dynamics = jnp.stack(
        [
            surface_elevation_cast,
            revised_zonal_velocity.astype(jnp.bfloat16),
            revised_meridional_velocity.astype(jnp.bfloat16),
        ],
        axis=1,
    )
    reordered = advance_dynamics.reshape(
        block_members, 3, tile_count, tile_columns, strips, strip_rows
    )
    reordered = jnp.transpose(reordered, (4, 2, 0, 1, 3, 5)).reshape(
        strips, tile_count, block_members, tile_cells
    )
    tile_block = lax.all_to_all(reordered, "mem", split_axis=0, concat_axis=2, tiled=True)[0]
    cells_here = observed_cell[0]
    values = jnp.take_along_axis(tile_block, cells_here[:, None, :], axis=2)
    observed_mean = jnp.sum(values, axis=1, dtype=jnp.float32) / members
    slot_index = jnp.arange(slot_count, dtype=jnp.int32)[None, :]
    live_slots = slot_index < observed_count[0][:, None]
    root_weight = jnp.sqrt(jnp.where(live_slots, 1.0 / error_variance[0], 0.0))
    spread = (
        root_weight[:, None, :] * (values.astype(jnp.float32) - observed_mean[:, None, :])
    ).astype(jnp.bfloat16)
    misfit = (root_weight * (observed_value[0] - observed_mean)).astype(jnp.bfloat16)
    spread_margin, misfit_margin = (
        padded_2(spread[None], (("mem", 0), ("band", 1)), 1),
        padded_2(misfit[None], (("mem", 0), ("band", 1)), 1),
    )
    gram_margin = jnp.einsum(
        "atko,atlo->atkl", spread_margin, spread_margin, preferred_element_type=jnp.float32
    )
    pull_margin = jnp.einsum(
        "atko,ato->atk", spread_margin, misfit_margin, preferred_element_type=jnp.float32
    )
    strip_here = lax.axis_index("mem")
    lower_valid = (strip_here > 0).astype(jnp.float32)
    upper_valid = (strip_here < strips - 1).astype(jnp.float32)
    strip_mask = (lower_valid, 1.0, upper_valid)
    total_gram = jnp.zeros((tile_count, members, members), jnp.float32)
    total_pull = jnp.zeros((tile_count, members), jnp.float32)
    for offset_lat in range(3):
        for offset_lon in range(3):
            factor = (
                neighbour_weight ** (abs(offset_lat - 1) + abs(offset_lon - 1))
                * strip_mask[offset_lat]
            )
            total_gram = (
                total_gram + factor * gram_margin[offset_lat, offset_lon : offset_lon + tile_count]
            )
            total_pull = (
                total_pull + factor * pull_margin[offset_lat, offset_lon : offset_lon + tile_count]
            )
    system = (members - 1) * jnp.eye(members, dtype=jnp.float32)[None] + total_gram
    frobenius = jnp.sqrt(jnp.sum(system * system, axis=(1, 2)))
    inverse_root = newton_schulz(system / frobenius[:, None, None])
    spread_map = inverse_root * (math.sqrt(members - 1) / jnp.sqrt(frobenius))[:, None, None]
    half_pull = jnp.einsum("tij,tj->ti", inverse_root, total_pull, precision=lax.Precision.HIGHEST)
    shift_weights = (
        jnp.einsum("tij,tj->ti", inverse_root, half_pull, precision=lax.Precision.HIGHEST)
        / frobenius[:, None]
    )
    weights = (spread_map + shift_weights[:, :, None]).astype(jnp.bfloat16)
    state_mean = jnp.sum(tile_block, axis=1, dtype=jnp.float32) / members
    anomaly = (tile_block.astype(jnp.float32) - state_mean[:, None, :]).astype(jnp.bfloat16)
    update = jnp.einsum("tjk,tjc->tkc", weights, anomaly, preferred_element_type=jnp.float32)
    analysed = (state_mean[:, None, :] + update).astype(jnp.bfloat16)
    returned = lax.all_to_all(analysed[None], "mem", split_axis=2, concat_axis=0, tiled=True)
    returned = returned.reshape(strips, tile_count, block_members, 3, tile_columns, strip_rows)
    return jnp.transpose(returned, (2, 3, 1, 4, 0, 5)).reshape(block_members, 3, columns, latitudes)


def solution(mesh):
    in_specs = (
        P("mem", None, "band", None),
        P("band", None),
        P("mem", "band", None),
        P("mem", "band", None),
        P("mem", "band", None),
        P("mem", "band"),
    )
    out_specs = P("mem", None, "band", None)
    return jax.shard_map(
        on_device, mesh=mesh, in_specs=in_specs, out_specs=out_specs, check_vma=False
    )
```

profile of v0, /device:TPU:0, one launch (start us, length us, event | category | flops | bytes accessed | tf_op | source)
XLA Modules:
  0.0 279.9 jit_solution(7164611219929606275)
XLA Ops:
  0.0 2.0 fusion.1
  2.1 5.1 %collective-permute-start = (bf16[32,1,160]{2,0,1:T(8,128)(2,1)S(1)}, bf16[32,1,160]{2,0,1:T(8,128)(2,1)S(1)}, u32[]{:S(2)}, u32[]{:S(2)}) collective-permute-start(bf16[32,1,160]{2,0,1:T(8,128)(2,1)S(1)} %get-tuple-element.15), channel_id=1, source_target_pairs={{1,0},{2,1},{3,2},{0,3},{5,4},{6,5},{7,6},{4,7},{9,8},{10,9},{11,1... | collective-permute-start | bytes 30728 | tf_op jit(solution)/shard_map/ppermute | solution.py:22
  7.6 1.0 collective-permute-done
  8.6 4.1 %collective-permute-done.1 = bf16[32,1,160]{2,0,1:T(8,128)(2,1)S(1)} collective-permute-done((bf16[32,1,160]{2,0,1:T(8,128)(2,1)S(1)}, bf16[32,1,160]{2,0,1:T(8,128)(2,1)S(1)}, u32[]{:S(2)}, u32[]{:S(2)}) %collective-permute-start.1) | collective-permute-done | bytes 10272 | tf_op jit(solution)/shard_map/ppermute | solution.py:20
  12.7 2.1 fusion.11
  14.9 3.8 %collective-permute-start.3 = (bf16[32,1,160]{2,0,1:T(8,128)(2,1)S(1)}, bf16[32,1,160]{2,0,1:T(8,128)(2,1)S(1)}, u32[]{:S(2)}, u32[]{:S(2)}) collective-permute-start(bf16[32,1,160]{2,0,1:T(8,128)(2,1)S(1)} %get-tuple-element.14), channel_id=1, source_target_pairs={{1,0},{2,1},{3,2},{0,3},{5,4},{6,5},{7,6},{4,7},{9,8},{10,9},{11,1... | collective-permute-start | bytes 30728 | tf_op jit(solution)/shard_map/ppermute | solution.py:22
  18.8 2.1 copy.30
  20.9 4.6 %stack.12 = bf16[32,1,2,30,8,20]{3,2,5,4,0,1:T(2,128)(2,1)S(1)} reshape(bf16[32,60,160]{1,2,0:T(8,128)(2,1)} %copy.30) | data formatting | bytes 1228800 | tf_op jit(solution)/shard_map/stack | solution.py:87
  25.4 1.5 maximum_convert_fusion
  27.1 1.6 copy-done.2
  28.7 2.6 fusion.3
  31.4 3.0 %copy.31 = bf16[32,60,160]{1,2,0:T(8,128)(2,1)} copy(bf16[32,60,160]{2,0,1:T(8,128)(2,1)} %get-tuple-element.9) | data formatting | bytes 1228800 | tf_op jit(solution)/shard_map/convert_element_type | solution.py:90
  34.4 5.6 %stack.13 = bf16[32,1,2,30,8,20]{3,2,5,4,0,1:T(2,128)(2,1)} reshape(bf16[32,60,160]{1,2,0:T(8,128)(2,1)} %copy.31) | data formatting | bytes 1228800 | tf_op jit(solution)/shard_map/stack | solution.py:87
  40.0 3.1 %copy.32 = bf16[32,60,160]{1,2,0:T(8,128)(2,1)} copy(bf16[32,60,160]{2,0,1:T(8,128)(2,1)} %get-tuple-element.10) | data formatting | bytes 1228800 | tf_op jit(solution)/shard_map/convert_element_type | solution.py:91
  43.1 5.6 %stack.14 = bf16[32,1,2,30,8,20]{3,2,5,4,0,1:T(2,128)(2,1)} reshape(bf16[32,60,160]{1,2,0:T(8,128)(2,1)} %copy.32) | data formatting | bytes 1228800 | tf_op jit(solution)/shard_map/stack | solution.py:87
  48.7 17.0 %maximum_bitcast_fusion = bf16[8,2,32,3,30,20]{4,1,5,0,2,3:T(2,128)(2,1)} fusion(bf16[32,1,2,30,8,20]{3,2,5,4,0,1:T(2,128)(2,1)} %stack.14, bf16[32,1,2,30,8,20]{3,2,5,4,0,1:T(2,128)(2,1)} %stack.13, bf16[32,1,2,30,8,20]{3,2,5,4,0,1:T(2,128)(2,1)S(1)} %stack.12), kind=kLoop, calls=%fused_computation.1 | loop fusion | flops 1843200 | bytes 3686400 | tf_op jit(solution)/shard_map/transpose | solution.py:98
  65.7 24.9 %copy.33 = bf16[8,2,32,3,30,20]{2,0,5,4,3,1:T(8,128)(2,1)} copy(bf16[8,2,32,3,30,20]{4,1,5,0,2,3:T(2,128)(2,1)} %maximum_bitcast_fusion) | data formatting | bytes 3686400 | tf_op jit(solution)/shard_map/transpose | solution.py:98
  90.6 9.1 %copy.34 = bf16[8,2,32,1800]{3,2,1,0:T(8,128)(2,1)} copy(bf16[8,2,32,1800]{2,0,3,1:T(8,128)(2,1)} %bitcast.114) | data formatting | bytes 3686400 | tf_op jit(solution)/shard_map/reshape | solution.py:98
  99.7 4.0 %all-to-all-start = ((bf16[8,2,32,1800]{3,2,1,0:T(8,128)(2,1)}), bf16[8,2,32,1800]{3,2,1,0:T(8,128)(2,1)S(1)}, u32[]{:S(2)}, u32[]{:S(2)}) async-start(bf16[8,2,32,1800]{3,2,1,0:T(8,128)(2,1)} %copy.34), calls=%async_computation | async-start | bytes 3932160 | tf_op jit(solution)/shard_map/all_to_all | solution.py:101
  103.8 25.0 %all-to-all-done = bf16[8,2,32,1800]{3,2,1,0:T(8,128)(2,1)S(1)} async-done(((bf16[8,2,32,1800]{3,2,1,0:T(8,128)(2,1)}), bf16[8,2,32,1800]{3,2,1,0:T(8,128)(2,1)S(1)}, u32[]{:S(2)}, u32[]{:S(2)}) %all-to-all-start) | async-done | bytes 1843232 | tf_op jit(solution)/shard_map/all_to_all | solution.py:101
  128.8 1.5 copy.35
  130.8 2.8 %copy.36 = bf16[2,256,1800]{1,2,0:T(8,128)(2,1)S(1)} copy(bf16[2,256,1800]{2,1,0:T(8,128)(2,1)} %bitcast.118) | data formatting | bytes 3686400 | tf_op jit(solution)/shard_map/squeeze | solution.py:101
  133.6 5.8 %gather_fusion = bf16[1024,256]{1,0:T(8,128)(2,1)S(1)} fusion(bf16[2,256,1800]{1,2,0:T(8,128)(2,1)S(1)} %copy.36, s32[1024]{0:T(1024)S(1)} %bitcast.113), kind=kCustom, calls=%fused_computation | custom fusion | bytes 1056768 | tf_op jit(solution)/shard_map/jit(take_along_axis)/gather | solution.py:103
  140.8 2.3 collective-permute-start.9
  143.0 1.9 convert_reduce_fusion
  144.9 7.6 %collective-permute-done.5 = bf16[1,2,256,512]{3,2,1,0:T(8,128)(2,1)S(1)} collective-permute-done((bf16[1,2,256,512]{3,2,1,0:T(8,128)(2,1)S(1)}, bf16[1,2,256,512]{3,2,1,0:T(8,128)(2,1)S(1)}, u32[]{:S(2)}, u32[]{:S(2)}) %collective-permute-start.5) | collective-permute-done | bytes 524320 | tf_op jit(solution)/shard_map/ppermute | solution.py:22
  152.5 1.1 collective-permute-done.4
  153.9 3.8 %collective-permute-start.7 = (bf16[3,1,256,512]{3,2,1,0:T(8,128)(2,1)S(1)}, bf16[3,1,256,512]{3,2,1,0:T(8,128)(2,1)S(1)}, u32[]{:S(2)}, u32[]{:S(2)}) collective-permute-start(bf16[3,1,256,512]{3,2,1,0:T(8,128)(2,1)S(1)} %get-tuple-element.12), channel_id=1, source_target_pairs={{1,0},{2,1},{3,2},{0,3},{5,4},{6,5},{7,6},{4,7},{9,8},{10,9},{11,1... | collective-permute-start | bytes 2359304 | tf_op jit(solution)/shard_map/ppermute | solution.py:22
  157.9 3.8 %collective-permute-start.11 = (bf16[3,1,512]{2,1,0:T(2,128)(2,1)S(1)}, bf16[3,1,512]{2,1,0:T(2,128)(2,1)S(1)}, u32[]{:S(2)}, u32[]{:S(2)}) collective-permute-start(bf16[3,1,512]{2,1,0:T(2,128)(2,1)S(1)} %get-tuple-element.18), channel_id=1, source_target_pairs={{1,0},{2,1},{3,2},{0,3},{5,4},{6,5},{7,6},{4,7},{9,8},{10,9},{11,1... | collective-permute-start | bytes 9224 | tf_op jit(solution)/shard_map/ppermute | solution.py:22
  161.7 29.6 %collective-permute-done.10 = bf16[3,1,512]{2,1,0:T(2,128)(2,1)S(1)} collective-permute-done((bf16[3,1,512]{2,1,0:T(2,128)(2,1)S(1)}, bf16[3,1,512]{2,1,0:T(2,128)(2,1)S(1)}, u32[]{:S(2)}, u32[]{:S(2)}) %collective-permute-start.10) | collective-permute-done | bytes 3104 | tf_op jit(solution)/shard_map/ppermute | solution.py:20
  191.4 1.3 fusion.58
  193.1 0.7 fusion.17
  193.9 0.7 fusion.35
  195.2 0.7 fusion.16
  195.9 0.7 fusion.65
  196.5 0.7 fusion.64
  197.2 0.7 fusion.15
  199.2 0.7 fusion.14
  199.8 0.7 fusion.68
  201.2 1.3 fusion.36
  202.5 0.7 fusion.13
  203.2 0.7 fusion.70
  205.0 2.2 fusion
  207.2 5.1 %copy.39 = bf16[1,2,256,1800]{3,1,0,2:T(2,128)(2,1)S(1)} copy(bf16[1,2,256,1800]{2,3,1,0:T(8,128)(2,1)} %fusion) | data formatting | bytes 3686400 | tf_op jit(solution)/shard_map/broadcast_in_dim | solution.py:154
  212.3 28.6 %all_to_all.30 = bf16[1,2,256,1800]{3,1,0,2:T(2,128)(2,1)S(1)} all-to-all(bf16[1,2,256,1800]{3,1,0,2:T(2,128)(2,1)S(1)} %copy.39), channel_id=1, replica_groups=mesh['mem'=8,'band'=4] {'mem'}, dimensions={2} | all-to-all | bytes 3686400 | tf_op jit(solution)/shard_map/all_to_all | solution.py:154
  241.1 7.6 %copy.41 = bf16[8,1,2,32,1800]{3,0,4,2,1:T(8,128)(2,1)} copy(bf16[8,1,2,32,1800]{4,3,0,2,1:T(8,128)(2,1)S(1)} %bitcast.117) | data formatting | bytes 3686400 | tf_op jit(solution)/shard_map/all_to_all | solution.py:154
  248.6 16.8 %copy.50 = bf16[32,3,2,30,8,20]{5,4,0,3,2,1:T(8,128)(2,1)} copy(bf16[32,3,2,30,8,20]{0,4,5,3,1,2:T(8,128)(2,1)} %bitcast.115) | data formatting | bytes 3686400 | tf_op jit(solution)/shard_map/reshape | solution.py:156
  265.4 14.5 %reshape.287 = bf16[32,3,60,160]{3,0,2,1:T(8,128)(2,1)} reshape(bf16[32,3,2,30,8,20]{5,4,0,3,2,1:T(8,128)(2,1)} %copy.50) | data formatting | bytes 3686400 | tf_op jit(solution)/shard_map/reshape | solution.py:156
  (62 shorter events, 7.5 us)
Async XLA Ops:
  2.1 6.5 %collective-permute-start = (bf16[32,1,160]{2,0,1:T(8,128)(2,1)S(1)}, bf16[32,1,160]{2,0,1:T(8,128)(2,1)S(1)}, u32[]{:S(2)}, u32[]{:S(2)}) collective-permute-start(bf16[32,1,160]{2,0,1:T(8,128)(2,1)S(1)} %get-tuple-element.15), channel_id=1, source_target_pairs={{1,0},{2,1},{3,2},{0,3},{5,4},{6,5},{7,6},{4,7},{9,8},{10,9},{11,1... | collective-permute-start | bytes 30728 | tf_op jit(solution)/shard_map/ppermute | solution.py:22
  7.2 5.5 %collective-permute-start.1 = (bf16[32,1,160]{2,0,1:T(8,128)(2,1)S(1)}, bf16[32,1,160]{2,0,1:T(8,128)(2,1)S(1)}, u32[]{:S(2)}, u32[]{:S(2)}) collective-permute-start(bf16[32,1,160]{2,0,1:T(8,128)(2,1)S(1)} %get-tuple-element.16), channel_id=1, source_target_pairs={{0,1},{1,2},{2,3},{3,0},{4,5},{5,6},{6,7},{7,4},{8,9},{9,10},{10,1... | collective-permute-start | bytes 30728 | tf_op jit(solution)/shard_map/ppermute | solution.py:20
  14.8 4.0 %copy-start.1 = (bf16[32,60,160]{2,0,1:T(8,128)(2,1)}, bf16[32,60,160]{2,0,1:T(8,128)(2,1)S(1)}, u32[]{:S(2)}) copy-start(bf16[32,60,160]{2,0,1:T(8,128)(2,1)S(1)} %fusion.11) | copy-start | bytes 1843204
  14.8 10.6 %collective-permute-start.2 = (bf16[32,1,160]{2,0,1:T(8,128)(2,1)S(1)}, bf16[32,1,160]{2,0,1:T(8,128)(2,1)S(1)}, u32[]{:S(2)}, u32[]{:S(2)}) collective-permute-start(bf16[32,1,160]{2,0,1:T(8,128)(2,1)S(1)} %get-tuple-element.13), channel_id=1, source_target_pairs={{0,1},{1,2},{2,3},{3,0},{4,5},{5,6},{6,7},{7,4},{8,9},{9,10},{10,1... | collective-permute-start | bytes 30728 | tf_op jit(solution)/shard_map/ppermute | solution.py:20
  14.9 10.5 %collective-permute-start.3 = (bf16[32,1,160]{2,0,1:T(8,128)(2,1)S(1)}, bf16[32,1,160]{2,0,1:T(8,128)(2,1)S(1)}, u32[]{:S(2)}, u32[]{:S(2)}) collective-permute-start(bf16[32,1,160]{2,0,1:T(8,128)(2,1)S(1)} %get-tuple-element.14), channel_id=1, source_target_pairs={{1,0},{2,1},{3,2},{0,3},{5,4},{6,5},{7,6},{4,7},{9,8},{10,9},{11,1... | collective-permute-start | bytes 30728 | tf_op jit(solution)/shard_map/ppermute | solution.py:22
  26.9 1.8 copy-start.2
  99.7 4.0 %copy-start.3 = (s32[1,2,512]{2,1,0:T(2,128)S(1)}, s32[1,2,512]{2,1,0:T(2,128)}, u32[]{:S(2)}) copy-start(s32[1,2,512]{2,1,0:T(2,128)} %param.8) | copy-start | bytes 12292
  99.7 29.1 %all-to-all-start = ((bf16[8,2,32,1800]{3,2,1,0:T(8,128)(2,1)}), bf16[8,2,32,1800]{3,2,1,0:T(8,128)(2,1)S(1)}, u32[]{:S(2)}, u32[]{:S(2)}) async-start(bf16[8,2,32,1800]{3,2,1,0:T(8,128)(2,1)} %copy.34), calls=%async_computation | async-start | bytes 3932160 | tf_op jit(solution)/shard_map/all_to_all | solution.py:101
  128.8 2.0 copy-start
  133.6 6.2 %copy-start.4 = (f32[1,2,512]{2,1,0:T(2,128)S(1)}, f32[1,2,512]{2,1,0:T(2,128)}, u32[]{:S(2)}) copy-start(f32[1,2,512]{2,1,0:T(2,128)} %param.10) | copy-start | bytes 12292
  133.6 6.2 %copy-start.6 = (s32[1,2]{1,0:T(1,128)S(1)}, s32[1,2]{1,0:T(1,128)}, u32[]{:S(2)}) copy-start(s32[1,2]{1,0:T(1,128)} %param.11) | copy-start | bytes 28
  139.5 1.2 copy-start.5
  140.1 12.4 %collective-permute-start.5 = (bf16[1,2,256,512]{3,2,1,0:T(8,128)(2,1)S(1)}, bf16[1,2,256,512]{3,2,1,0:T(8,128)(2,1)S(1)}, u32[]{:S(2)}, u32[]{:S(2)}) collective-permute-start(bf16[1,2,256,512]{3,2,1,0:T(8,128)(2,1)S(1)} %multiply_convert_fusion), channel_id=1, source_target_pairs={{4,0},{8,4},{12,8},{16,12},{20,16},{24,20},{28,24},{0,28},{5,1},{9... | collective-permute-start | bytes 1572872 | tf_op jit(solution)/shard_map/ppermute | solution.py:22
  140.1 13.4 %collective-permute-start.4 = (bf16[1,2,256,512]{3,2,1,0:T(8,128)(2,1)S(1)}, bf16[1,2,256,512]{3,2,1,0:T(8,128)(2,1)S(1)}, u32[]{:S(2)}, u32[]{:S(2)}) collective-permute-start(bf16[1,2,256,512]{3,2,1,0:T(8,128)(2,1)S(1)} %multiply_convert_fusion), channel_id=1, source_target_pairs={{0,4},{4,8},{8,12},{12,16},{16,20},{20,24},{24,28},{28,0},{1,5},{5... | collective-permute-start | bytes 1572872 | tf_op jit(solution)/shard_map/ppermute | solution.py:20
  140.8 17.0 %collective-permute-start.9 = (bf16[1,2,512]{2,1,0:T(2,128)(2,1)S(1)}, bf16[1,2,512]{2,1,0:T(2,128)(2,1)S(1)}, u32[]{:S(2)}, u32[]{:S(2)}) collective-permute-start(bf16[1,2,512]{2,1,0:T(2,128)(2,1)S(1)} %fusion.45), channel_id=1, source_target_pairs={{4,0},{8,4},{12,8},{16,12},{20,16},{24,20},{28,24},{0,28},{5,1},{9... | collective-permute-start | bytes 6152 | tf_op jit(solution)/shard_map/ppermute | solution.py:22
  143.0 14.7 %collective-permute-start.8 = (bf16[1,2,512]{2,1,0:T(2,128)(2,1)S(1)}, bf16[1,2,512]{2,1,0:T(2,128)(2,1)S(1)}, u32[]{:S(2)}, u32[]{:S(2)}) collective-permute-start(bf16[1,2,512]{2,1,0:T(2,128)(2,1)S(1)} %fusion.45), channel_id=1, source_target_pairs={{0,4},{4,8},{8,12},{12,16},{16,20},{20,24},{24,28},{28,0},{1,5},{5... | collective-permute-start | bytes 6152 | tf_op jit(solution)/shard_map/ppermute | solution.py:20
  153.9 37.5 %collective-permute-start.6 = (bf16[3,1,256,512]{3,2,1,0:T(8,128)(2,1)S(1)}, bf16[3,1,256,512]{3,2,1,0:T(8,128)(2,1)S(1)}, u32[]{:S(2)}, u32[]{:S(2)}) collective-permute-start(bf16[3,1,256,512]{3,2,1,0:T(8,128)(2,1)S(1)} %get-tuple-element.11), channel_id=1, source_target_pairs={{0,1},{1,2},{2,3},{3,0},{4,5},{5,6},{6,7},{7,4},{8,9},{9,10},{10,1... | collective-permute-start | bytes 2359304 | tf_op jit(solution)/shard_map/ppermute | solution.py:20
  153.9 37.4 %collective-permute-start.7 = (bf16[3,1,256,512]{3,2,1,0:T(8,128)(2,1)S(1)}, bf16[3,1,256,512]{3,2,1,0:T(8,128)(2,1)S(1)}, u32[]{:S(2)}, u32[]{:S(2)}) collective-permute-start(bf16[3,1,256,512]{3,2,1,0:T(8,128)(2,1)S(1)} %get-tuple-element.12), channel_id=1, source_target_pairs={{1,0},{2,1},{3,2},{0,3},{5,4},{6,5},{7,6},{4,7},{9,8},{10,9},{11,1... | collective-permute-start | bytes 2359304 | tf_op jit(solution)/shard_map/ppermute | solution.py:22
  157.8 33.5 %collective-permute-start.10 = (bf16[3,1,512]{2,1,0:T(2,128)(2,1)S(1)}, bf16[3,1,512]{2,1,0:T(2,128)(2,1)S(1)}, u32[]{:S(2)}, u32[]{:S(2)}) collective-permute-start(bf16[3,1,512]{2,1,0:T(2,128)(2,1)S(1)} %get-tuple-element.17), channel_id=1, source_target_pairs={{0,1},{1,2},{2,3},{3,0},{4,5},{5,6},{6,7},{7,4},{8,9},{9,10},{10,1... | collective-permute-start | bytes 9224 | tf_op jit(solution)/shard_map/ppermute | solution.py:20
  157.9 33.4 %collective-permute-start.11 = (bf16[3,1,512]{2,1,0:T(2,128)(2,1)S(1)}, bf16[3,1,512]{2,1,0:T(2,128)(2,1)S(1)}, u32[]{:S(2)}, u32[]{:S(2)}) collective-permute-start(bf16[3,1,512]{2,1,0:T(2,128)(2,1)S(1)} %get-tuple-element.18), channel_id=1, source_target_pairs={{1,0},{2,1},{3,2},{0,3},{5,4},{6,5},{7,6},{4,7},{9,8},{10,9},{11,1... | collective-permute-start | bytes 9224 | tf_op jit(solution)/shard_map/ppermute | solution.py:22
where the time goes:
time: 282 us; the launch traced here: 280 us
  local copies, waits for them, and re-layouts  115 us (41%)
  waiting for transfers between devices  68.4 us (24%)
  other arithmetic  28.9 us (10%)
  blocking collectives  28.6 us (10%)
  starting transfers between devices  23.5 us (8%)
  matrix products  15.1 us (5%)
    ppermute x6, waiting for transfers between devices, padded_2(): lax.ppermute(tail, axis, [(i, (i + 1) % count) for i in range(count)])  34.8 us
    reshape x2, local copies, waits for them, and re-layouts, on_device(): jnp.transpose(returned, (2, 3, 1, 4, 0, 5))  31.3 us
    all_to_all x1, blocking collectives, on_device(): lax.all_to_all(analysed[None], 'mem', split_axis=2, concat_axis=0, tiled=...  28.6 us
    all_to_all x1, waiting for transfers between devices, on_device(): lax.all_to_all(reordered, 'mem', split_axis=0, concat_axis=2, tiled=True)[0]  25 us
    transpose x1, local copies, waits for them, and re-layouts, on_device(): jnp.transpose(reordered, (4, 2, 0, 1, 3, 5))  24.9 us
    ppermute x6, starting transfers between devices, padded_2(): lax.ppermute(head, axis, [((i + 1) % count, i) for i in range(count)])  18.8 us
    transpose x1, other arithmetic, on_device(): jnp.transpose(reordered, (4, 2, 0, 1, 3, 5))  17 us
    another operation x3, local copies, waits for them, and re-layouts, on_device(): jnp.stack([surface_elevation_cast, revised_zonal_velocity.astype(jnp.bflo...  15.8 us
  transfers between devices with their start and end apart: 13, of which 6 were waited for; matrix products, arithmetic and copies ran while one was open for 3% of the time, Pallas kernels for 0%

commit v1 on v0

--- a/solution.py
+++ b/solution.py
@@ -1,13 +1,48 @@
+import functools
 import math
 import jax
 import jax.numpy as jnp
 from jax import lax
 from jax.sharding import PartitionSpec as P
+from jax.lax import axis_index, axis_size, ppermute
 
 SWEEPS = 5
 half_step = 0.1
 coriolis_scale = 0.3
 neighbour_weight = 0.75
+
+
+def list_the_series_all(x_local, join_dim, array_here):
+    high = x_local.shape
+    value_now = x_local.reshape(
+        *high[:join_dim], array_here, high[join_dim] // array_here, *high[join_dim + 1 :]
+    )
+    e_now = jnp.moveaxis(value_now, join_dim, 0)
+    return e_now
+
+
+def advance_the_stocks(state, dim_i):
+    e_next = list(state.shape[1:])
+    e_next[dim_i] *= state.shape[0]
+    before = jnp.moveaxis(state, 0, dim_i).reshape(e_next)
+    return before
+
+
+def _save_shifts_all(xin, my_data, mesh_name, packet):
+    shaped, current_arr = (axis_size(mesh_name), axis_index(mesh_name))
+    top = list_the_series_all(xin, my_data, shaped)
+    by_place = [top[current_arr]]
+    for dev in tuple(range(1, shaped)):
+        odd = top[current_arr ^ dev]
+        by_place.append(
+            ppermute(odd, axis_name=mesh_name, perm=[(jj, jj ^ dev) for jj in range(shaped)])
+        )
+    top = jnp.stack(by_place, axis=0)[current_arr ^ jnp.arange(shaped)]
+    taken_in = advance_the_stocks(top, packet)
+    return taken_in
+
+
+render_local_data = functools.partial(_save_shifts_all, my_data=2, mesh_name="mem", packet=0)
 
 
 def padded_2(cells, sides, width):
@@ -151,7 +186,7 @@
     anomaly = (tile_block.astype(jnp.float32) - state_mean[:, None, :]).astype(jnp.bfloat16)
     update = jnp.einsum("tjk,tjc->tkc", weights, anomaly, preferred_element_type=jnp.float32)
     analysed = (state_mean[:, None, :] + update).astype(jnp.bfloat16)
-    returned = lax.all_to_all(analysed[None], "mem", split_axis=2, concat_axis=0, tiled=True)
+    returned = render_local_data(analysed[None])
     returned = returned.reshape(strips, tile_count, block_members, 3, tile_columns, strip_rows)
     return jnp.transpose(returned, (2, 3, 1, 4, 0, 5)).reshape(block_members, 3, columns, latitudes)
 

time: 282 us -> 281 us (level)
  blocking collectives: 28.6 us -> 0 us
  waiting for transfers between devices: 68.4 us -> 85.1 us
  starting transfers between devices: 23.5 us -> 31.8 us
    all_to_all x1 -> x0, blocking collectives: 28.6 us -> none  [on_device(): lax.all_to_all(analysed[None], 'mem', split_axis=2, concat_axis=0, tiled=...]
    ppermute x0 -> x7, waiting for transfers between devices: none -> 17.5 us  [_save_shifts_all(): ppermute(odd, axis_name=mesh_name, perm=[(jj, jj ^ dev) for jj in range(s...]
    gather x0 -> x2, local copies, waits for them, and re-layouts: none -> 9.93 us  [_save_shifts_all(): top = jnp.stack(by_place, axis=0)[current_arr ^ jnp.arange(shaped)]]
    ppermute x0 -> x7, starting transfers between devices: none -> 8.31 us  [_save_shifts_all(): ppermute(odd, axis_name=mesh_name, perm=[(jj, jj ^ dev) for jj in range(s...]
    all_to_all x2 -> x0, local copies, waits for them, and re-layouts: 7.75 us -> none  [on_device(): lax.all_to_all(analysed[None], 'mem', split_axis=2, concat_axis=0, tiled=...]
    broadcast_in_dim x1 -> x0, local copies, waits for them, and re-layouts: 5.08 us -> none  [on_device(): analysed[None]]
  transfers between devices with their start and end apart: 13 -> 20, of which waited for: 6 -> 9; matrix products, arithmetic and copies ran while one was open for 3% -> 4% of each run, Pallas kernels for 0% -> 0%
where the time goes in v1:
time: 281 us; the launch traced here: 279 us
  local copies, waits for them, and re-layouts  116 us (41%)
  waiting for transfers between devices  85.1 us (30%)
  starting transfers between devices  31.8 us (11%)
  other arithmetic  29.7 us (11%)
  matrix products  15.1 us (5%)
    ppermute x6, waiting for transfers between devices, padded_2(): lax.ppermute(tail, axis, [(i, (i + 1) % count) for i in range(count)])  34.8 us
    reshape x2, local copies, waits for them, and re-layouts, on_device(): jnp.transpose(returned, (2, 3, 1, 4, 0, 5))  31.3 us
    transpose x1, local copies, waits for them, and re-layouts, on_device(): jnp.transpose(reordered, (4, 2, 0, 1, 3, 5))  24.9 us
    all_to_all x1, waiting for transfers between devices, on_device(): lax.all_to_all(reordered, 'mem', split_axis=0, concat_axis=2, tiled=True)[0]  24.2 us
    ppermute x6, starting transfers between devices, padded_2(): lax.ppermute(head, axis, [((i + 1) % count, i) for i in range(count)])  18.8 us
    ppermute x7, waiting for transfers between devices, _save_shifts_all(): ppermute(odd, axis_name=mesh_name, perm=[(jj, jj ^ dev) for jj in range(s...  17.5 us
    transpose x1, other arithmetic, on_device(): jnp.transpose(reordered, (4, 2, 0, 1, 3, 5))  17.1 us
    another operation x3, local copies, waits for them, and re-layouts, on_device(): jnp.stack([surface_elevation_cast, revised_zonal_velocity.astype(jnp.bflo...  15.8 us
  transfers between devices with their start and end apart: 20, of which 9 were waited for; matrix products, arithmetic and copies ran while one was open for 4% of the time, Pallas kernels for 0%

profile of v1, /device:TPU:0, one launch (start us, length us, event | category | flops | bytes accessed | tf_op | source)
XLA Modules:
  0.0 278.8 jit_solution(3285994092311827240)
XLA Ops:
  0.0 2.0 fusion
  2.1 5.1 %collective-permute-start = (bf16[32,1,160]{2,0,1:T(8,128)(2,1)S(1)}, bf16[32,1,160]{2,0,1:T(8,128)(2,1)S(1)}, u32[]{:S(2)}, u32[]{:S(2)}) collective-permute-start(bf16[32,1,160]{2,0,1:T(8,128)(2,1)S(1)} %get-tuple-element.22), channel_id=1, source_target_pairs={{1,0},{2,1},{3,2},{0,3},{5,4},{6,5},{7,6},{4,7},{9,8},{10,9},{11,1... | collective-permute-start | bytes 30728 | tf_op jit(solution)/shard_map/ppermute | solution.py:57
  7.6 1.0 collective-permute-done
  8.6 4.1 %collective-permute-done.1 = bf16[32,1,160]{2,0,1:T(8,128)(2,1)S(1)} collective-permute-done((bf16[32,1,160]{2,0,1:T(8,128)(2,1)S(1)}, bf16[32,1,160]{2,0,1:T(8,128)(2,1)S(1)}, u32[]{:S(2)}, u32[]{:S(2)}) %collective-permute-start.1) | collective-permute-done | bytes 10272 | tf_op jit(solution)/shard_map/ppermute | solution.py:55
  12.7 2.1 fusion.10
  14.9 3.8 %collective-permute-start.3 = (bf16[32,1,160]{2,0,1:T(8,128)(2,1)S(1)}, bf16[32,1,160]{2,0,1:T(8,128)(2,1)S(1)}, u32[]{:S(2)}, u32[]{:S(2)}) collective-permute-start(bf16[32,1,160]{2,0,1:T(8,128)(2,1)S(1)} %get-tuple-element.21), channel_id=1, source_target_pairs={{1,0},{2,1},{3,2},{0,3},{5,4},{6,5},{7,6},{4,7},{9,8},{10,9},{11,1... | collective-permute-start | bytes 30728 | tf_op jit(solution)/shard_map/ppermute | solution.py:57
  18.8 2.1 copy.30
  20.9 4.6 %stack.36 = bf16[32,1,2,30,8,20]{3,2,5,4,0,1:T(2,128)(2,1)S(1)} reshape(bf16[32,60,160]{1,2,0:T(8,128)(2,1)} %copy.30) | data formatting | bytes 1228800 | tf_op jit(solution)/shard_map/stack | solution.py:122
  25.4 1.5 maximum_convert_fusion
  27.1 1.6 copy-done.2
  28.7 2.7 fusion.2
  31.4 3.0 %copy.31 = bf16[32,60,160]{1,2,0:T(8,128)(2,1)} copy(bf16[32,60,160]{2,0,1:T(8,128)(2,1)} %get-tuple-element.9) | data formatting | bytes 1228800 | tf_op jit(solution)/shard_map/convert_element_type | solution.py:125
  34.4 5.6 %stack.37 = bf16[32,1,2,30,8,20]{3,2,5,4,0,1:T(2,128)(2,1)} reshape(bf16[32,60,160]{1,2,0:T(8,128)(2,1)} %copy.31) | data formatting | bytes 1228800 | tf_op jit(solution)/shard_map/stack | solution.py:122
  40.1 3.1 %copy.32 = bf16[32,60,160]{1,2,0:T(8,128)(2,1)} copy(bf16[32,60,160]{2,0,1:T(8,128)(2,1)} %get-tuple-element.10) | data formatting | bytes 1228800 | tf_op jit(solution)/shard_map/convert_element_type | solution.py:126
  43.2 5.6 %stack.38 = bf16[32,1,2,30,8,20]{3,2,5,4,0,1:T(2,128)(2,1)} reshape(bf16[32,60,160]{1,2,0:T(8,128)(2,1)} %copy.32) | data formatting | bytes 1228800 | tf_op jit(solution)/shard_map/stack | solution.py:122
  48.8 17.1 %maximum_bitcast_fusion = bf16[8,2,32,3,30,20]{4,1,5,0,2,3:T(2,128)(2,1)} fusion(bf16[32,1,2,30,8,20]{3,2,5,4,0,1:T(2,128)(2,1)} %stack.38, bf16[32,1,2,30,8,20]{3,2,5,4,0,1:T(2,128)(2,1)} %stack.37, bf16[32,1,2,30,8,20]{3,2,5,4,0,1:T(2,128)(2,1)S(1)} %stack.36), kind=kLoop, calls=%fused_computation.2 | loop fusion | flops 1843200 | bytes 3686400 | tf_op jit(solution)/shard_map/transpose | solution.py:133
  65.9 24.9 %copy.33 = bf16[8,2,32,3,30,20]{2,0,5,4,3,1:T(8,128)(2,1)} copy(bf16[8,2,32,3,30,20]{4,1,5,0,2,3:T(2,128)(2,1)} %maximum_bitcast_fusion) | data formatting | bytes 3686400 | tf_op jit(solution)/shard_map/transpose | solution.py:133
  90.8 9.1 %copy.34 = bf16[8,2,32,1800]{3,2,1,0:T(8,128)(2,1)} copy(bf16[8,2,32,1800]{2,0,3,1:T(8,128)(2,1)} %bitcast.143) | data formatting | bytes 3686400 | tf_op jit(solution)/shard_map/reshape | solution.py:133
  99.8 4.0 %all-to-all-start = ((bf16[8,2,32,1800]{3,2,1,0:T(8,128)(2,1)}), bf16[8,2,32,1800]{3,2,1,0:T(8,128)(2,1)S(1)}, u32[]{:S(2)}, u32[]{:S(2)}) async-start(bf16[8,2,32,1800]{3,2,1,0:T(8,128)(2,1)} %copy.34), calls=%async_computation | async-start | bytes 3932160 | tf_op jit(solution)/shard_map/all_to_all | solution.py:136
  104.7 24.2 %all-to-all-done = bf16[8,2,32,1800]{3,2,1,0:T(8,128)(2,1)S(1)} async-done(((bf16[8,2,32,1800]{3,2,1,0:T(8,128)(2,1)}), bf16[8,2,32,1800]{3,2,1,0:T(8,128)(2,1)S(1)}, u32[]{:S(2)}, u32[]{:S(2)}) %all-to-all-start) | async-done | bytes 1843232 | tf_op jit(solution)/shard_map/all_to_all | solution.py:136
  128.9 1.5 copy.35
  130.9 2.8 %copy.36 = bf16[2,256,1800]{1,2,0:T(8,128)(2,1)S(1)} copy(bf16[2,256,1800]{2,1,0:T(8,128)(2,1)} %bitcast.148) | data formatting | bytes 3686400 | tf_op jit(solution)/shard_map/squeeze | solution.py:136
  133.8 5.8 %gather_fusion.1 = bf16[1024,256]{1,0:T(8,128)(2,1)S(1)} fusion(bf16[2,256,1800]{1,2,0:T(8,128)(2,1)S(1)} %copy.36, s32[1024]{0:T(1024)S(1)} %bitcast.142), kind=kCustom, calls=%fused_computation.1 | custom fusion | bytes 1056768 | tf_op jit(solution)/shard_map/jit(take_along_axis)/gather | solution.py:138
  140.9 2.3 collective-permute-start.9
  143.1 1.9 convert_reduce_fusion
  145.0 7.6 %collective-permute-done.5 = bf16[1,2,256,512]{3,2,1,0:T(8,128)(2,1)S(1)} collective-permute-done((bf16[1,2,256,512]{3,2,1,0:T(8,128)(2,1)S(1)}, bf16[1,2,256,512]{3,2,1,0:T(8,128)(2,1)S(1)}, u32[]{:S(2)}, u32[]{:S(2)}) %collective-permute-start.5) | collective-permute-done | bytes 524320 | tf_op jit(solution)/shard_map/ppermute | solution.py:57
  152.6 1.1 collective-permute-done.4
  154.1 3.8 %collective-permute-start.7 = (bf16[3,1,256,512]{3,2,1,0:T(8,128)(2,1)S(1)}, bf16[3,1,256,512]{3,2,1,0:T(8,128)(2,1)S(1)}, u32[]{:S(2)}, u32[]{:S(2)}) collective-permute-start(bf16[3,1,256,512]{3,2,1,0:T(8,128)(2,1)S(1)} %get-tuple-element.19), channel_id=1, source_target_pairs={{1,0},{2,1},{3,2},{0,3},{5,4},{6,5},{7,6},{4,7},{9,8},{10,9},{11,1... | collective-permute-start | bytes 2359304 | tf_op jit(solution)/shard_map/ppermute | solution.py:57
  158.0 3.8 %collective-permute-start.11 = (bf16[3,1,512]{2,1,0:T(2,128)(2,1)S(1)}, bf16[3,1,512]{2,1,0:T(2,128)(2,1)S(1)}, u32[]{:S(2)}, u32[]{:S(2)}) collective-permute-start(bf16[3,1,512]{2,1,0:T(2,128)(2,1)S(1)} %get-tuple-element.25), channel_id=1, source_target_pairs={{1,0},{2,1},{3,2},{0,3},{5,4},{6,5},{7,6},{4,7},{9,8},{10,9},{11,1... | collective-permute-start | bytes 9224 | tf_op jit(solution)/shard_map/ppermute | solution.py:57
  161.8 29.6 %collective-permute-done.10 = bf16[3,1,512]{2,1,0:T(2,128)(2,1)S(1)} collective-permute-done((bf16[3,1,512]{2,1,0:T(2,128)(2,1)S(1)}, bf16[3,1,512]{2,1,0:T(2,128)(2,1)S(1)}, u32[]{:S(2)}, u32[]{:S(2)}) %collective-permute-start.10) | collective-permute-done | bytes 3104 | tf_op jit(solution)/shard_map/ppermute | solution.py:55
  191.5 1.3 fusion.58
  193.3 0.7 fusion.16
  201.3 1.3 fusion.35
  205.2 2.2 add_convert_fusion
  207.4 2.8 copy.39
  210.3 1.9 collective-permute-start.18
  212.2 1.6 collective-permute-start.16
  213.8 0.9 collective-permute-start.15
  214.8 1.5 collective-permute-done.12
  216.3 2.3 collective-permute-start.13
  218.6 9.9 %collective-permute-done.13 = bf16[1,2,32,1800]{3,2,1,0:T(8,128)(2,1)S(1)} collective-permute-done((bf16[1,2,32,1800]{3,2,1,0:T(8,128)(2,1)S(1)}, bf16[1,2,32,1800]{3,2,1,0:T(8,128)(2,1)S(1)}, u32[]{:S(2)}, u32[]{:S(2)}) %collective-permute-start.13) | collective-permute-done | bytes 230432 | tf_op jit(solution)/shard_map/ppermute | solution.py:38
  228.5 1.6 collective-permute-start.14
  230.1 6.1 %collective-permute-done.14 = bf16[1,2,32,1800]{3,2,1,0:T(8,128)(2,1)S(1)} collective-permute-done((bf16[1,2,32,1800]{3,2,1,0:T(8,128)(2,1)S(1)}, bf16[1,2,32,1800]{3,2,1,0:T(8,128)(2,1)S(1)}, u32[]{:S(2)}, u32[]{:S(2)}) %collective-permute-start.14) | collective-permute-done | bytes 230432 | tf_op jit(solution)/shard_map/ppermute | solution.py:38
  236.3 1.3 copy-done.3
  237.6 2.4 gather_fusion
  240.0 7.6 %copy.40 = bf16[8,2,32,1800]{2,0,3,1:T(8,128)(2,1)} copy(bf16[8,2,32,1800]{3,2,1,0:T(8,128)(2,1)S(1)} %gather_fusion) | data formatting | bytes 3686400 | tf_op jit(solution)/shard_map/gather | solution.py:40
  247.5 16.8 %copy.49 = bf16[32,3,2,30,8,20]{5,4,0,3,2,1:T(8,128)(2,1)} copy(bf16[32,3,2,30,8,20]{0,4,5,3,1,2:T(8,128)(2,1)} %bitcast.144) | data formatting | bytes 3686400 | tf_op jit(solution)/shard_map/reshape | solution.py:191
  264.3 14.5 %reshape.324 = bf16[32,3,60,160]{3,0,2,1:T(8,128)(2,1)} reshape(bf16[32,3,2,30,8,20]{5,4,0,3,2,1:T(8,128)(2,1)} %copy.49) | data formatting | bytes 3686400 | tf_op jit(solution)/shard_map/reshape | solution.py:191
  (90 shorter events, 14.4 us)
Async XLA Ops:
  2.1 6.5 %collective-permute-start = (bf16[32,1,160]{2,0,1:T(8,128)(2,1)S(1)}, bf16[32,1,160]{2,0,1:T(8,128)(2,1)S(1)}, u32[]{:S(2)}, u32[]{:S(2)}) collective-permute-start(bf16[32,1,160]{2,0,1:T(8,128)(2,1)S(1)} %get-tuple-element.22), channel_id=1, source_target_pairs={{1,0},{2,1},{3,2},{0,3},{5,4},{6,5},{7,6},{4,7},{9,8},{10,9},{11,1... | collective-permute-start | bytes 30728 | tf_op jit(solution)/shard_map/ppermute | solution.py:57
  7.2 5.5 %collective-permute-start.1 = (bf16[32,1,160]{2,0,1:T(8,128)(2,1)S(1)}, bf16[32,1,160]{2,0,1:T(8,128)(2,1)S(1)}, u32[]{:S(2)}, u32[]{:S(2)}) collective-permute-start(bf16[32,1,160]{2,0,1:T(8,128)(2,1)S(1)} %get-tuple-element.23), channel_id=1, source_target_pairs={{0,1},{1,2},{2,3},{3,0},{4,5},{5,6},{6,7},{7,4},{8,9},{9,10},{10,1... | collective-permute-start | bytes 30728 | tf_op jit(solution)/shard_map/ppermute | solution.py:55
  14.8 4.0 %copy-start.1 = (bf16[32,60,160]{2,0,1:T(8,128)(2,1)}, bf16[32,60,160]{2,0,1:T(8,128)(2,1)S(1)}, u32[]{:S(2)}) copy-start(bf16[32,60,160]{2,0,1:T(8,128)(2,1)S(1)} %fusion.10) | copy-start | bytes 1843204
  14.8 10.6 %collective-permute-start.2 = (bf16[32,1,160]{2,0,1:T(8,128)(2,1)S(1)}, bf16[32,1,160]{2,0,1:T(8,128)(2,1)S(1)}, u32[]{:S(2)}, u32[]{:S(2)}) collective-permute-start(bf16[32,1,160]{2,0,1:T(8,128)(2,1)S(1)} %get-tuple-element.20), channel_id=1, source_target_pairs={{0,1},{1,2},{2,3},{3,0},{4,5},{5,6},{6,7},{7,4},{8,9},{9,10},{10,1... | collective-permute-start | bytes 30728 | tf_op jit(solution)/shard_map/ppermute | solution.py:55
  14.9 10.5 %collective-permute-start.3 = (bf16[32,1,160]{2,0,1:T(8,128)(2,1)S(1)}, bf16[32,1,160]{2,0,1:T(8,128)(2,1)S(1)}, u32[]{:S(2)}, u32[]{:S(2)}) collective-permute-start(bf16[32,1,160]{2,0,1:T(8,128)(2,1)S(1)} %get-tuple-element.21), channel_id=1, source_target_pairs={{1,0},{2,1},{3,2},{0,3},{5,4},{6,5},{7,6},{4,7},{9,8},{10,9},{11,1... | collective-permute-start | bytes 30728 | tf_op jit(solution)/shard_map/ppermute | solution.py:57
  26.9 1.8 copy-start.2
  99.8 4.0 %copy-start.5 = (s32[1,2,512]{2,1,0:T(2,128)S(1)}, s32[1,2,512]{2,1,0:T(2,128)}, u32[]{:S(2)}) copy-start(s32[1,2,512]{2,1,0:T(2,128)} %param.8) | copy-start | bytes 12292
  99.8 29.1 %all-to-all-start = ((bf16[8,2,32,1800]{3,2,1,0:T(8,128)(2,1)}), bf16[8,2,32,1800]{3,2,1,0:T(8,128)(2,1)S(1)}, u32[]{:S(2)}, u32[]{:S(2)}) async-start(bf16[8,2,32,1800]{3,2,1,0:T(8,128)(2,1)} %copy.34), calls=%async_computation | async-start | bytes 3932160 | tf_op jit(solution)/shard_map/all_to_all | solution.py:136
  128.9 2.0 copy-start
  133.7 6.2 %copy-start.6 = (f32[1,2,512]{2,1,0:T(2,128)S(1)}, f32[1,2,512]{2,1,0:T(2,128)}, u32[]{:S(2)}) copy-start(f32[1,2,512]{2,1,0:T(2,128)} %param.10) | copy-start | bytes 12292
  133.8 6.2 %copy-start.8 = (s32[1,2]{1,0:T(1,128)S(1)}, s32[1,2]{1,0:T(1,128)}, u32[]{:S(2)}) copy-start(s32[1,2]{1,0:T(1,128)} %param.11) | copy-start | bytes 28
  139.6 1.2 copy-start.7
  140.2 12.4 %collective-permute-start.5 = (bf16[1,2,256,512]{3,2,1,0:T(8,128)(2,1)S(1)}, bf16[1,2,256,512]{3,2,1,0:T(8,128)(2,1)S(1)}, u32[]{:S(2)}, u32[]{:S(2)}) collective-permute-start(bf16[1,2,256,512]{3,2,1,0:T(8,128)(2,1)S(1)} %multiply_convert_fusion), channel_id=1, source_target_pairs={{4,0},{8,4},{12,8},{16,12},{20,16},{24,20},{28,24},{0,28},{5,1},{9... | collective-permute-start | bytes 1572872 | tf_op jit(solution)/shard_map/ppermute | solution.py:57
  140.3 13.4 %collective-permute-start.4 = (bf16[1,2,256,512]{3,2,1,0:T(8,128)(2,1)S(1)}, bf16[1,2,256,512]{3,2,1,0:T(8,128)(2,1)S(1)}, u32[]{:S(2)}, u32[]{:S(2)}) collective-permute-start(bf16[1,2,256,512]{3,2,1,0:T(8,128)(2,1)S(1)} %multiply_convert_fusion), channel_id=1, source_target_pairs={{0,4},{4,8},{8,12},{12,16},{16,20},{20,24},{24,28},{28,0},{1,5},{5... | collective-permute-start | bytes 1572872 | tf_op jit(solution)/shard_map/ppermute | solution.py:55
  140.9 17.0 %collective-permute-start.9 = (bf16[1,2,512]{2,1,0:T(2,128)(2,1)S(1)}, bf16[1,2,512]{2,1,0:T(2,128)(2,1)S(1)}, u32[]{:S(2)}, u32[]{:S(2)}) collective-permute-start(bf16[1,2,512]{2,1,0:T(2,128)(2,1)S(1)} %fusion.44), channel_id=1, source_target_pairs={{4,0},{8,4},{12,8},{16,12},{20,16},{24,20},{28,24},{0,28},{5,1},{9... | collective-permute-start | bytes 6152 | tf_op jit(solution)/shard_map/ppermute | solution.py:57
  143.1 14.8 %collective-permute-start.8 = (bf16[1,2,512]{2,1,0:T(2,128)(2,1)S(1)}, bf16[1,2,512]{2,1,0:T(2,128)(2,1)S(1)}, u32[]{:S(2)}, u32[]{:S(2)}) collective-permute-start(bf16[1,2,512]{2,1,0:T(2,128)(2,1)S(1)} %fusion.44), channel_id=1, source_target_pairs={{0,4},{4,8},{8,12},{12,16},{16,20},{20,24},{24,28},{28,0},{1,5},{5... | collective-permute-start | bytes 6152 | tf_op jit(solution)/shard_map/ppermute | solution.py:55
  154.0 37.5 %collective-permute-start.6 = (bf16[3,1,256,512]{3,2,1,0:T(8,128)(2,1)S(1)}, bf16[3,1,256,512]{3,2,1,0:T(8,128)(2,1)S(1)}, u32[]{:S(2)}, u32[]{:S(2)}) collective-permute-start(bf16[3,1,256,512]{3,2,1,0:T(8,128)(2,1)S(1)} %get-tuple-element.18), channel_id=1, source_target_pairs={{0,1},{1,2},{2,3},{3,0},{4,5},{5,6},{6,7},{7,4},{8,9},{9,10},{10,1... | collective-permute-start | bytes 2359304 | tf_op jit(solution)/shard_map/ppermute | solution.py:55
  154.1 37.4 %collective-permute-start.7 = (bf16[3,1,256,512]{3,2,1,0:T(8,128)(2,1)S(1)}, bf16[3,1,256,512]{3,2,1,0:T(8,128)(2,1)S(1)}, u32[]{:S(2)}, u32[]{:S(2)}) collective-permute-start(bf16[3,1,256,512]{3,2,1,0:T(8,128)(2,1)S(1)} %get-tuple-element.19), channel_id=1, source_target_pairs={{1,0},{2,1},{3,2},{0,3},{5,4},{6,5},{7,6},{4,7},{9,8},{10,9},{11,1... | collective-permute-start | bytes 2359304 | tf_op jit(solution)/shard_map/ppermute | solution.py:57
  157.9 33.5 %collective-permute-start.10 = (bf16[3,1,512]{2,1,0:T(2,128)(2,1)S(1)}, bf16[3,1,512]{2,1,0:T(2,128)(2,1)S(1)}, u32[]{:S(2)}, u32[]{:S(2)}) collective-permute-start(bf16[3,1,512]{2,1,0:T(2,128)(2,1)S(1)} %get-tuple-element.24), channel_id=1, source_target_pairs={{0,1},{1,2},{2,3},{3,0},{4,5},{5,6},{6,7},{7,4},{8,9},{9,10},{10,1... | collective-permute-start | bytes 9224 | tf_op jit(solution)/shard_map/ppermute | solution.py:55
  158.0 33.4 %collective-permute-start.11 = (bf16[3,1,512]{2,1,0:T(2,128)(2,1)S(1)}, bf16[3,1,512]{2,1,0:T(2,128)(2,1)S(1)}, u32[]{:S(2)}, u32[]{:S(2)}) collective-permute-start(bf16[3,1,512]{2,1,0:T(2,128)(2,1)S(1)} %get-tuple-element.25), channel_id=1, source_target_pairs={{1,0},{2,1},{3,2},{0,3},{5,4},{6,5},{7,6},{4,7},{9,8},{10,9},{11,1... | collective-permute-start | bytes 9224 | tf_op jit(solution)/shard_map/ppermute | solution.py:57
  191.5 1.3 copy-start.4
  210.3 26.0 %collective-permute-start.18 = (bf16[1,2,32,1800]{3,2,1,0:T(8,128)(2,1)S(1)}, bf16[1,2,32,1800]{3,2,1,0:T(8,128)(2,1)S(1)}, u32[]{:S(2)}, u32[]{:S(2)}) collective-permute-start(bf16[1,2,32,1800]{3,2,1,0:T(8,128)(2,1)S(1)} %get-tuple-element.11), channel_id=1, source_target_pairs={{0,28},{4,24},{8,20},{12,16},{16,12},{20,8},{24,4},{28,0},{1,29},{... | collective-permute-start | bytes 691208 | tf_op jit(solution)/shard_map/ppermute | solution.py:38
  212.2 24.0 %collective-permute-start.17 = (bf16[1,2,32,1800]{3,2,1,0:T(8,128)(2,1)S(1)}, bf16[1,2,32,1800]{3,2,1,0:T(8,128)(2,1)S(1)}, u32[]{:S(2)}, u32[]{:S(2)}) collective-permute-start(bf16[1,2,32,1800]{3,2,1,0:T(8,128)(2,1)S(1)} %get-tuple-element.12), channel_id=1, source_target_pairs={{0,24},{4,28},{8,16},{12,20},{16,8},{20,12},{24,0},{28,4},{1,25},{... | collective-permute-start | bytes 691208 | tf_op jit(solution)/shard_map/ppermute | solution.py:38
  212.2 23.9 %collective-permute-start.16 = (bf16[1,2,32,1800]{3,2,1,0:T(8,128)(2,1)S(1)}, bf16[1,2,32,1800]{3,2,1,0:T(8,128)(2,1)S(1)}, u32[]{:S(2)}, u32[]{:S(2)}) collective-permute-start(bf16[1,2,32,1800]{3,2,1,0:T(8,128)(2,1)S(1)} %get-tuple-element.13), channel_id=1, source_target_pairs={{0,20},{4,16},{8,28},{12,24},{16,4},{20,0},{24,12},{28,8},{1,21},{... | collective-permute-start | bytes 691208 | tf_op jit(solution)/shard_map/ppermute | solution.py:38
  213.8 22.3 %collective-permute-start.15 = (bf16[1,2,32,1800]{3,2,1,0:T(8,128)(2,1)S(1)}, bf16[1,2,32,1800]{3,2,1,0:T(8,128)(2,1)S(1)}, u32[]{:S(2)}, u32[]{:S(2)}) collective-permute-start(bf16[1,2,32,1800]{3,2,1,0:T(8,128)(2,1)S(1)} %get-tuple-element.14), channel_id=1, source_target_pairs={{0,16},{4,20},{8,24},{12,28},{16,0},{20,4},{24,8},{28,12},{1,17},{... | collective-permute-start | bytes 691208 | tf_op jit(solution)/shard_map/ppermute | solution.py:38
  214.8 1.5 collective-permute-start.12
  216.3 12.2 %collective-permute-start.13 = (bf16[1,2,32,1800]{3,2,1,0:T(8,128)(2,1)S(1)}, bf16[1,2,32,1800]{3,2,1,0:T(8,128)(2,1)S(1)}, u32[]{:S(2)}, u32[]{:S(2)}) collective-permute-start(bf16[1,2,32,1800]{3,2,1,0:T(8,128)(2,1)S(1)} %get-tuple-element.16), channel_id=1, source_target_pairs={{0,8},{4,12},{8,0},{12,4},{16,24},{20,28},{24,16},{28,20},{1,9},{5... | collective-permute-start | bytes 691208 | tf_op jit(solution)/shard_map/ppermute | solution.py:38
  228.5 7.6 %collective-permute-start.14 = (bf16[1,2,32,1800]{3,2,1,0:T(8,128)(2,1)S(1)}, bf16[1,2,32,1800]{3,2,1,0:T(8,128)(2,1)S(1)}, u32[]{:S(2)}, u32[]{:S(2)}) collective-permute-start(bf16[1,2,32,1800]{3,2,1,0:T(8,128)(2,1)S(1)} %get-tuple-element.15), channel_id=1, source_target_pairs={{0,12},{4,8},{8,4},{12,0},{16,28},{20,24},{24,20},{28,16},{1,13},{... | collective-permute-start | bytes 691208 | tf_op jit(solution)/shard_map/ppermute | solution.py:38
  236.3 1.3 copy-start.3
